TPU v7x, 256 devices: a whole 4x4x8 slice. The times are simulated.
256 devices in a mesh: replica: 32 (over x, z), tensor: 8 (over y, core).
Axes of the slice: x: 4, y: 4, z: 8, core: 2. Of those that a mesh axis runs over, the one named last changes fastest.
Arguments:
- tokens: bfloat16 [96, 2048], P('replica'), may hold values from -0.8984375 to 0.8984375
- long_tokens: bfloat16 [32, 2048], P('replica'), may hold values from -0.8984375 to 0.8984375
- cache: bfloat16 [2, 2, 96, 2048, 8, 128], P(None, None, 'replica', None, 'tensor')
- long_request_cache: bfloat16 [2, 2, 32, 2, 2048, 8, 128], P(None, None, 'replica', None, None, 'tensor')
- lengths: int32 [96], replicated, may hold values from 1 to 2047, as said below
- long_lengths: int32 [32], replicated, may hold values from 2049 to 4095, as said below
- norm_gain: float32 [2, 2048], replicated, may hold values from 0.1 to 1.9
- q_gain: float32 [2, 128], replicated, may hold values from 0.1 to 1.9
- k_gain: float32 [2, 128], replicated, may hold values from 0.1 to 1.9
- w_query: bfloat16 [2, 2048, 2048], P(None, None, 'tensor'), may hold values from -0.125 to 0.125
- key_weight: bfloat16 [2, 2048, 1024], P(None, None, 'tensor'), may hold values from -0.125 to 0.125
- value_weight: bfloat16 [2, 2048, 1024], P(None, None, 'tensor'), may hold values from -0.125 to 0.125
- w_out: bfloat16 [2, 2048, 2048], P(None, 'tensor'), may hold values from -0.125 to 0.125
Outputs:
- out_hidden: float32 [96, 2048], P('replica')
- out_long: float32 [32, 2048], P('replica')
- moved_cache: bfloat16 [32, 2, 2, 2048, 8, 128], P('replica', None, None, None, 'tensor')
Inputs may be any that keep to these rules, and one draw needn't show every extreme that they name: `lengths`: cached length of each request; some request has 2047 in every draw. `long_lengths`: cached length of each long request, always past 2048; some long request has 4095 in every draw.
All inputs are finite; a program needn't handle non-finite values.
Results may differ from a plain program's by a relative error of at most 0.028.
Values may be sent and summed in bfloat16 or wider, within the bound.
No kernel may reach another device: no remote copies, remote signals or barrier semaphores. Data moves between devices by JAX's collectives and lax.ppermute only.
A program may use at most 64 MiB of HBM per device.

v0:
```python
import jax
import jax.numpy as jnp
from jax import lax
from jax.sharding import PartitionSpec as P

EPSILON = 1e-06
ROPE_BASE = 1000000.0
NEGATIVE = -1e30


def shifted(block, axis, distance):
    devices = range(lax.axis_size(axis))
    route = [((i - distance) % len(devices), i) for i in devices]
    return lax.ppermute(block, axis, route)


def partner_2(value, axis, apart):
    mask = 2**apart
    pairs = [(source, source ^ mask) for source in range(lax.axis_size(axis))]
    return lax.ppermute(value, axis, pairs)


def rms_scale(values, gain_row):
    return (
        values * lax.rsqrt(jnp.mean(values * values, axis=-1, keepdims=True) + EPSILON) * gain_row
    )


def rotate(values, places):
    head_width = values.shape[-1]
    halfway = head_width // 2
    inverse = ROPE_BASE ** (-2.0 * jnp.arange(halfway, dtype=jnp.float32) / head_width)
    angles = places.astype(jnp.float32)[:, None, None] * inverse
    cosine = jnp.cos(angles)
    sine_of = jnp.sin(angles)
    leading = values[..., :halfway]
    trailing = values[..., halfway:]
    return jnp.concatenate(
        [leading * cosine - trailing * sine_of, trailing * cosine + leading * sine_of], axis=-1
    )


def project(hidden, gain_row, w_query, key_weight, value_weight, query_gain, key_gain, places):
    head_width = query_gain.shape[-1]
    count_rows = hidden.shape[0]
    normed = rms_scale(hidden.astype(jnp.float32), gain_row).astype(jnp.bfloat16)
    queries = jnp.dot(normed, w_query, preferred_element_type=jnp.float32).reshape(
        count_rows, -1, head_width
    )
    keys_new = jnp.dot(normed, key_weight, preferred_element_type=jnp.float32).reshape(
        count_rows, -1, head_width
    )
    values_new = (
        jnp.dot(normed, value_weight, preferred_element_type=jnp.float32)
        .reshape(count_rows, -1, head_width)
        .astype(jnp.bfloat16)
    )
    queries = rotate(rms_scale(queries, query_gain), places).astype(jnp.bfloat16)
    keys_new = rotate(rms_scale(keys_new, key_gain), places).astype(jnp.bfloat16)
    return (queries, keys_new, values_new)


def own_terms(queries, key_new):
    head_width = queries.shape[-1]
    grouped = queries.reshape(key_new.shape[0], -1, head_width)
    return jnp.einsum(
        "kgd,kd->kg", grouped, key_new, preferred_element_type=jnp.float32
    ) * head_width ** (-0.5)


def masked_scores(queries, key_rows, visible):
    head_width = queries.shape[-1]
    grouped = queries.reshape(key_rows.shape[1], -1, head_width)
    scores = jnp.einsum(
        "kgd,tkd->kgt", grouped, key_rows, preferred_element_type=jnp.float32
    ) * head_width ** (-0.5)
    return jnp.where(visible[None, None, :], scores, NEGATIVE)


def attend(queries, key_rows, value_rows, visible, key_new, value_new):
    scores = masked_scores(queries, key_rows, visible)
    own_score = own_terms(queries, key_new)
    highest = jnp.maximum(jnp.max(scores, axis=-1), own_score)
    weights = jnp.exp(scores - highest[..., None])
    own_weight = jnp.exp(own_score - highest)
    denominator = jnp.sum(weights, axis=-1) + own_weight
    summed = jnp.einsum(
        "kgt,tkd->kgd", weights.astype(jnp.bfloat16), value_rows, preferred_element_type=jnp.float32
    )
    own_rounded = lax.optimization_barrier(own_weight.astype(jnp.bfloat16)).astype(jnp.float32)
    summed = summed + own_rounded[..., None] * value_new.astype(jnp.float32)[:, None, :]
    return (summed / denominator[..., None]).reshape(queries.shape).astype(jnp.bfloat16)


def partial_attend(queries, key_rows, value_rows, visible):
    scores = masked_scores(queries, key_rows, visible)
    highest = jnp.max(scores, axis=-1)
    weights = jnp.exp(scores - highest[..., None])
    summed = jnp.einsum(
        "kgt,tkd->kgd", weights.astype(jnp.bfloat16), value_rows, preferred_element_type=jnp.float32
    )
    return (highest, jnp.sum(weights, axis=-1), summed)


def combine(one_side, far_side):
    highest = jnp.maximum(one_side[0], far_side[0])
    factor_here = jnp.exp(one_side[0] - highest)
    factor_far = jnp.exp(far_side[0] - highest)
    totals = one_side[1] * factor_here + far_side[1] * factor_far
    summed = one_side[2] * factor_here[..., None] + far_side[2] * factor_far[..., None]
    return (highest, totals, summed)


def close_with_own(state_in, queries, key_new, value_new):
    own_score = own_terms(queries, key_new)
    highest = jnp.maximum(state_in[0], own_score)
    factor_here = jnp.exp(state_in[0] - highest)
    own_weight = jnp.exp(own_score - highest)
    denominator = state_in[1] * factor_here + own_weight
    own_rounded = lax.optimization_barrier(own_weight.astype(jnp.bfloat16)).astype(jnp.float32)
    summed = (
        state_in[2] * factor_here[..., None]
        + own_rounded[..., None] * value_new.astype(jnp.float32)[:, None, :]
    )
    return (summed / denominator[..., None]).reshape(queries.shape).astype(jnp.bfloat16)


def local(
    tokens,
    long_tokens,
    cache,
    long_request_cache,
    lengths,
    long_lengths,
    norm_gain,
    q_gain,
    k_gain,
    w_query,
    key_weight,
    value_weight,
    w_out,
):
    groups = lax.axis_size("replica")
    group_at = lax.axis_index("replica")
    per_group = tokens.shape[0]
    resident = per_group - 1
    layers = cache.shape[0]
    positions = jnp.arange(cache.shape[3])
    half_len = long_request_cache.shape[4]
    partner = (group_at + groups // 2) % groups
    local_len = lax.dynamic_slice_in_dim(lengths, group_at * per_group, per_group)
    arrived_len = lax.dynamic_index_in_dim(
        lengths, partner * per_group + resident, 0, keepdims=False
    )
    parity = group_at % 2
    pair_len = lax.dynamic_slice_in_dim(long_lengths, group_at - parity, 2)
    arrived_cache, arrived_token = shifted(
        (cache[:, :, resident], tokens[resident:]), "replica", groups // 2
    )
    hidden = jnp.concatenate([tokens[:resident], arrived_token], axis=0)
    places = jnp.concatenate([local_len[:resident], arrived_len[None]])
    visible = positions[None, :] < places[:, None]
    partner_token = partner_2(long_tokens, "replica", 0)
    long_hidden = jnp.where(
        parity == 0,
        jnp.concatenate([long_tokens, partner_token], axis=0),
        jnp.concatenate([partner_token, long_tokens], axis=0),
    )
    offsets = parity * half_len + jnp.arange(half_len)
    long_visible = offsets[None, :] < pair_len[:, None]
    main_rows = hidden.shape[0]
    fresh_rows = []
    for layer_at in range(layers):
        queries, keys_new, values_new = project(
            hidden,
            norm_gain[layer_at],
            w_query[layer_at],
            key_weight[layer_at],
            value_weight[layer_at],
            q_gain[layer_at],
            k_gain[layer_at],
            places,
        )
        staying = jax.vmap(attend)(
            queries[:resident],
            cache[layer_at, 0, :resident],
            cache[layer_at, 1, :resident],
            visible[:resident],
            keys_new[:resident],
            values_new[:resident],
        )
        incoming = attend(
            queries[resident],
            arrived_cache[layer_at, 0],
            arrived_cache[layer_at, 1],
            visible[resident],
            keys_new[resident],
            values_new[resident],
        )
        attended = jnp.concatenate([staying, incoming[None]], axis=0)
        fresh_rows.append(jnp.stack([keys_new[resident], values_new[resident]]))
        long_queries, long_keys, long_values = project(
            long_hidden,
            norm_gain[layer_at],
            w_query[layer_at],
            key_weight[layer_at],
            value_weight[layer_at],
            q_gain[layer_at],
            k_gain[layer_at],
            pair_len,
        )
        state_here = jax.vmap(partial_attend)(
            long_queries,
            long_request_cache[layer_at, 0, 0],
            long_request_cache[layer_at, 1, 0],
            long_visible,
        )
        state_far = partner_2(state_here, "replica", 0)
        merged = combine(state_here, state_far)
        long_attended = jax.vmap(close_with_own)(merged, long_queries, long_keys, long_values)
        stacked = jnp.concatenate([attended, long_attended], axis=0)
        heads_out = jnp.dot(
            stacked.reshape(stacked.shape[0], -1),
            w_out[layer_at],
            preferred_element_type=jnp.float32,
        )
        summed = lax.psum(heads_out, "tensor")
        carried = jnp.concatenate([hidden, long_hidden], axis=0).astype(jnp.float32) + summed
        if layer_at + 1 < layers:
            carried = carried.astype(jnp.bfloat16)
        hidden = carried[:main_rows]
        long_hidden = carried[main_rows:]
    fresh_all = jnp.stack(fresh_rows)
    moved_here = lax.dynamic_update_slice_in_dim(
        arrived_cache, fresh_all[:, :, None], arrived_len, axis=2
    )
    long_out = lax.dynamic_slice_in_dim(long_hidden, parity, 1)
    return (hidden, long_out, moved_here[None])


def solution(mesh):
    return jax.shard_map(
        local,
        mesh=mesh,
        in_specs=(
            P("replica", None),
            P("replica", None),
            P(None, None, "replica", None, "tensor", None),
            P(None, None, "replica", None, None, "tensor", None),
            P(),
            P(),
            P(),
            P(),
            P(),
            P(None, None, "tensor"),
            P(None, None, "tensor"),
            P(None, None, "tensor"),
            P(None, "tensor", None),
        ),
        out_specs=(
            P("replica", None),
            P("replica", None),
            P("replica", None, None, None, "tensor", None),
        ),
        check_vma=False,
    )
```

profile of v0, /device:TPU:64, one launch (start us, length us, event | category | flops | bytes accessed | tf_op | source)
XLA Modules:
  0.0 137.5 jit_solution(526159633632751661)
XLA Ops:
  1.4 3.1 %collective-permute-start = (bf16[1,2048]{1,0:T(2,128)(2,1)S(1)}, bf16[1,2048]{1,0:T(2,128)(2,1)S(1)}, u32[]{:S(2)}, u32[]{:S(2)}) collective-permute-start(bf16[1,2048]{1,0:T(2,128)(2,1)S(1)} %slice.220), channel_id=1, source_target_pairs={{128,0},{136,8},{144,16},{152,24},{160,32},{168,40},{176,48},{184,... | collective-permute-start | bytes 12296 | tf_op jit(solution)/shard_map/ppermute | solution.py:14
  4.5 1.9 %collective-permute-start.1 = (bf16[1,2048]{1,0:T(2,128)(2,1)}, bf16[1,2048]{1,0:T(2,128)(2,1)S(1)}, u32[]{:S(2)}, u32[]{:S(2)}) collective-permute-start(bf16[1,2048]{1,0:T(2,128)(2,1)} %param.14), channel_id=1, source_target_pairs={{0,8},{8,0},{16,24},{24,16},{32,40},{40,32},{48,56},{56,48},{64,72... | collective-permute-start | bytes 12296 | tf_op jit(solution)/shard_map/ppermute | solution.py:20
  6.5 3.0 %slice_bitcast_fusion = bf16[2,2,2048,1,128]{4,2,1,0,3:T(8,128)(2,1)} fusion(bf16[2,2,3,2048,1,128]{5,3,4,2,1,0:T(8,128)(2,1)} %param.15), kind=kLoop, calls=%fused_computation.12 | loop fusion | bytes 4194304 | tf_op jit(solution)/shard_map/squeeze | solution.py:158
  11.9 1.7 %slice_bitcast_fusion.18 = (bf16[256,2048]{0,1:T(8,128)(2,1)S(1)}, bf16[256,2048]{0,1:T(8,128)(2,1)S(1)}) fusion(bf16[2,2048,256]{2,1,0:T(8,128)(2,1)} %param.22), kind=kLoop, calls=%fused_computation.56 | loop fusion | bytes 4194304 | tf_op jit(solution)/shard_map/dot_general | solution.py:47
  17.2 1.4 %multiply_reduce_fusion.5 = (f32[3]{0:T(128)S(1)}, f32[3,128]{1,0:T(4,128)S(1)}) fusion(bf16[2,2048,128]{2,1,0:T(8,128)(2,1)} %param.23, f32[2048]{0:T(1024)S(1)} %bitcast.414, f32[3]{0:T(128)S(1)} %add_rsqrt_fusion.11, bf16[1,2048]{1,0:T(2,128)(2,1)S(1)} %collective-permute-done, bf16[2,2048]{1,0:T(2,128)(2,1)S(1)} %slice.219), kind=kOutput, calls=%fused_computation.200 | convolution fusion | flops 1616637 | bytes 546328 | tf_op jit(solution)/shard_map/dot_general | solution.py:50
  21.1 1.7 %fusion.203 = (f32[2,2]{1,0:T(2,128)S(1)}, f32[2,2,2048]{2,1,0:T(2,128)S(1)}) fusion(bf16[2,2,1,2,2048,1,128]{6,4,3,5,2,1,0:T(8,128)(2,1)} %bitcast.441, bf16[2,2,128]{2,0,1:T(2,128)(2,1)S(1)} %pad_maximum_fusion.4, pred[2,2048]{1,0:T(4,128)(4,1)S(1)} %broadcast_compare_fusion), kind=kOutput, calls=%fused_computation.350 | convolution fusion | flops 2121724 | bytes 1086480 | tf_op jit(solution)/shard_map/vmap(kgd,tkd->kgt)/dot_general | solution.py:74
  23.0 1.5 %fusion.23 = f32[2,2,128]{2,1,0:T(2,128)S(1)} fusion(bf16[2,2,1,2,2048,1,128]{6,4,3,5,2,1,0:T(8,128)(2,1)} %bitcast.442, f32[2,2,2048]{2,1,0:T(2,128)S(1)} %get-tuple-element.64, f32[2,2]{1,0:T(2,128)S(1)} %get-tuple-element.63), kind=kOutput, calls=%fused_computation.45 | convolution fusion | flops 2113536 | bytes 1083408 | tf_op jit(solution)/shard_map/vmap(kgt,tkd->kgd)/dot_general | solution.py:99
  25.7 1.8 %fusion.205 = (f32[2,2]{1,0:T(2,128)S(1)}, f32[2,2,2048]{2,1,0:T(2,128)S(1)}) fusion(bf16[2,2,3,2048,1,128]{5,3,2,4,1,0:T(8,128)(2,1)} %bitcast.404, bf16[2,2,128]{2,0,1:T(2,128)(2,1)S(1)} %fusion.143, pred[2,2048]{1,0:T(4,128)(4,1)S(1)} %bitcast.420), kind=kOutput, calls=%fused_computation.352 | convolution fusion | flops 2121724 | bytes 1086480 | tf_op jit(solution)/shard_map/vmap(kgd,tkd->kgt)/dot_general | solution.py:74
  27.7 1.5 %fusion.11 = bf16[1,2,2,128]{3,2,1,0:T(2,128)(2,1)S(1)} fusion(bf16[2,2,3,2048,1,128]{5,3,2,4,1,0:T(8,128)(2,1)} %bitcast.405, f32[2,2,2048]{2,1,0:T(2,128)S(1)} %get-tuple-element.72, f32[2,2]{1,0:T(2,128)S(1)} %multiply_maximum_fusion.1, f32[2,2]{1,0:T(2,128)S(1)} %get-tuple-element.42, f32[2,128]{1,0:T(2,128)S(1)} %slice_convert_fusion.1, ...), kind=kOutput, calls=%fused_computation.22 | convolution fusion | flops 2115584 | bytes 1083440 | tf_op jit(solution)/shard_map/vmap(kgt,tkd->kgd)/dot_general | solution.py:87
  29.5 1.9 %collective-permute-start.3 = (f32[2,1,2]{2,0,1:T(2,128)S(1)}, f32[2,1,2]{2,0,1:T(2,128)S(1)}, u32[]{:S(2)}, u32[]{:S(2)}) collective-permute-start(f32[2,1,2]{2,0,1:T(2,128)S(1)} %bitcast.428), channel_id=1, source_target_pairs={{0,8},{8,0},{16,24},{24,16},{32,40},{40,32},{48,56},{56,48},{64,72... | collective-permute-start | bytes 56 | tf_op jit(solution)/shard_map/ppermute | solution.py:20
  33.1 1.9 %collective-permute-done.4 = f32[2,1,2,128]{3,2,0,1:T(2,128)S(1)} collective-permute-done((f32[2,1,2,128]{3,2,0,1:T(2,128)S(1)}, f32[2,1,2,128]{3,2,0,1:T(2,128)S(1)}, u32[]{:S(2)}, u32[]{:S(2)}) %collective-permute-start.4) | collective-permute-done | bytes 2080 | tf_op jit(solution)/shard_map/ppermute | solution.py:20
  35.1 23.1 %collective-permute-done.2 = bf16[2,2,2048,1,128]{4,2,1,0,3:T(8,128)(2,1)} collective-permute-done((bf16[2,2,2048,1,128]{4,2,1,0,3:T(8,128)(2,1)}, bf16[2,2,2048,1,128]{4,2,1,0,3:T(8,128)(2,1)}, u32[]{:S(2)}, u32[]{:S(2)}) %collective-permute-start.2) | collective-permute-done | bytes 2097184 | tf_op jit(solution)/shard_map/ppermute | solution.py:14
  58.1 1.4 %fusion.204 = (f32[2]{0:T(128)S(1)}, f32[2,2048]{1,0:T(2,128)S(1)}) fusion(bf16[2,2,2048,1,128]{4,2,1,0,3:T(8,128)(2,1)} %collective-permute-done.2, bf16[1,2,128]{2,0,1:T(2,128)(2,1)S(1)} %pad_maximum_fusion.2, pred[2048]{0:T(1024)(128)(4,1)S(1)} %slice_reduce_fusion), kind=kOutput, calls=%fused_computation.351 | convolution fusion | flops 1060862 | bytes 543240 | tf_op jit(solution)/shard_map/kgd,tkd->kgt/dot_general | solution.py:74
  61.3 24.8 %psum.14 = f32[5,2048]{1,0:T(8,128)S(1)} all-reduce(f32[5,2048]{1,0:T(8,128)S(1)} %fusion.26), channel_id=1, replica_groups=mesh['replica'=32,'tensor'=8] {'tensor'}, use_global_device_ids=true, to_apply=%region_12.13 | all-reduce | flops 10240 | bytes 81920 | tf_op jit(solution)/shard_map/psum | solution.py:227
  86.5 1.4 %convolution_convert_fusion = bf16[3,128]{1,0:T(4,128)(2,1)S(1)} fusion(bf16[2,2048,128]{2,1,0:T(8,128)(2,1)} %param.24, f32[2048]{0:T(1024)S(1)} %bitcast.408, f32[3]{0:T(128)S(1)} %add_rsqrt_fusion.7, bf16[5,2048]{1,0:T(8,128)(2,1)S(1)} %add_convert_fusion), kind=kOutput, calls=%fused_computation.17 | convolution fusion | flops 1597824 | bytes 550144 | tf_op jit(solution)/shard_map/dot_general | solution.py:54
  89.2 1.4 %multiply_reduce_fusion.6 = (f32[2]{0:T(128)S(1)}, f32[2,128]{1,0:T(2,128)S(1)}) fusion(bf16[2,2048,128]{2,1,0:T(8,128)(2,1)} %param.23, f32[2]{0:T(128)S(1)} %add_rsqrt_fusion.5, f32[2048]{0:T(1024)S(1)} %bitcast.410, bf16[5,2048]{1,0:T(8,128)(2,1)S(1)} %add_convert_fusion), kind=kOutput, calls=%fused_computation.244 | convolution fusion | flops 1065470 | bytes 542216 | tf_op jit(solution)/shard_map/dot_general | solution.py:50
  91.5 1.4 %multiply_reduce_fusion.3 = (f32[3]{0:T(128)S(1)}, f32[3,128]{1,0:T(4,128)S(1)}) fusion(bf16[2,2048,128]{2,1,0:T(8,128)(2,1)} %param.23, f32[2048]{0:T(1024)S(1)} %bitcast.413, f32[3]{0:T(128)S(1)} %add_rsqrt_fusion.7, bf16[5,2048]{1,0:T(8,128)(2,1)S(1)} %add_convert_fusion), kind=kOutput, calls=%fused_computation.194 | convolution fusion | flops 1598205 | bytes 550924 | tf_op jit(solution)/shard_map/dot_general | solution.py:50
  95.3 1.7 %fusion.208 = (f32[2,2]{1,0:T(2,128)S(1)}, f32[2,2,2048]{2,1,0:T(2,128)S(1)}) fusion(bf16[2,2,3,2048,1,128]{5,3,2,4,1,0:T(8,128)(2,1)} %bitcast.406, bf16[2,2,128]{2,0,1:T(2,128)(2,1)S(1)} %fusion.142, pred[2,2048]{1,0:T(4,128)(4,1)S(1)} %bitcast.421), kind=kOutput, calls=%fused_computation.355 | convolution fusion | flops 2121724 | bytes 1086480 | tf_op jit(solution)/shard_map/vmap(kgd,tkd->kgt)/dot_general | solution.py:74
  97.2 1.4 %fusion.207 = (f32[2]{0:T(128)S(1)}, f32[2,2048]{1,0:T(2,128)S(1)}) fusion(bf16[2,2,2048,1,128]{4,2,1,0,3:T(8,128)(2,1)} %collective-permute-done.2, bf16[1,2,128]{2,0,1:T(2,128)(2,1)S(1)} %pad_maximum_fusion.1, pred[2048]{0:T(1024)(128)(4,1)S(1)} %slice_reduce_fusion), kind=kOutput, calls=%fused_computation.354 | convolution fusion | flops 1060862 | bytes 543240 | tf_op jit(solution)/shard_map/kgd,tkd->kgt/dot_general | solution.py:74
  101.7 1.5 %fusion.10 = bf16[1,2,2,128]{3,2,1,0:T(2,128)(2,1)S(1)} fusion(bf16[2,2,3,2048,1,128]{5,3,2,4,1,0:T(8,128)(2,1)} %bitcast.407, f32[2,2,2048]{2,1,0:T(2,128)S(1)} %get-tuple-element.86, f32[2,2]{1,0:T(2,128)S(1)} %multiply_maximum_fusion, f32[2,2]{1,0:T(2,128)S(1)} %get-tuple-element.36, f32[2,128]{1,0:T(2,128)S(1)} %slice_convert_fusion, ...), kind=kOutput, calls=%fused_computation.21 | convolution fusion | flops 2115584 | bytes 1083440 | tf_op jit(solution)/shard_map/vmap(kgt,tkd->kgd)/dot_general | solution.py:87
  103.7 1.6 %collective-permute-start.6 = (f32[2,1,2]{2,0,1:T(2,128)S(1)}, f32[2,1,2]{2,0,1:T(2,128)S(1)}, u32[]{:S(2)}, u32[]{:S(2)}) collective-permute-start(f32[2,1,2]{2,0,1:T(2,128)S(1)} %bitcast.426), channel_id=1, source_target_pairs={{0,8},{8,0},{16,24},{24,16},{32,40},{40,32},{48,56},{56,48},{64,72... | collective-permute-start | bytes 56 | tf_op jit(solution)/shard_map/ppermute | solution.py:20
  107.3 1.6 %collective-permute-done.7 = f32[2,1,2,128]{3,2,0,1:T(2,128)S(1)} collective-permute-done((f32[2,1,2,128]{3,2,0,1:T(2,128)S(1)}, f32[2,1,2,128]{3,2,0,1:T(2,128)S(1)}, u32[]{:S(2)}, u32[]{:S(2)}) %collective-permute-start.7) | collective-permute-done | bytes 2080 | tf_op jit(solution)/shard_map/ppermute | solution.py:20
  109.3 23.9 %psum.15 = f32[5,2048]{1,0:T(8,128)S(1)} all-reduce(f32[5,2048]{1,0:T(8,128)S(1)} %fusion.24), channel_id=1, replica_groups=mesh['replica'=32,'tensor'=8] {'tensor'}, use_global_device_ids=true, to_apply=%region_25.26 | all-reduce | flops 10240 | bytes 81920 | tf_op jit(solution)/shard_map/psum | solution.py:227
  134.5 3.0 %copy.125 = bf16[1,2,2,2048,1,128]{5,3,4,2,1,0:T(8,128)(2,1)} copy(bf16[1,2,2,2048,1,128]{5,3,4,2,1,0:T(8,128)(2,1)} %dynamic_update_slice.4) | data formatting | bytes 4194304
  (158 shorter events, 24.6 us)
Async XLA Ops:
  1.4 8.7 %copy-start.9 = (s32[96]{0:T(128)S(1)}, s32[96]{0:T(128)}, u32[]{:S(2)}) copy-start(s32[96]{0:T(128)} %param.17) | copy-start | bytes 1156
  1.4 9.3 %copy-start.4 = (f32[2,128]{1,0:T(2,128)S(1)}, f32[2,128]{1,0:T(2,128)}, u32[]{:S(2)}) copy-start(f32[2,128]{1,0:T(2,128)} %param.20) | copy-start | bytes 3076
  1.4 9.3 %copy-start.5 = (f32[2,128]{1,0:T(2,128)S(1)}, f32[2,128]{1,0:T(2,128)}, u32[]{:S(2)}) copy-start(f32[2,128]{1,0:T(2,128)} %param.21) | copy-start | bytes 3076
  1.4 10.0 %copy-start.6 = (s32[32]{0:T(128)S(1)}, s32[32]{0:T(128)}, u32[]{:S(2)}) copy-start(s32[32]{0:T(128)} %param.18) | copy-start | bytes 388
  1.4 10.4 %copy-start.1 = (f32[2,2048]{1,0:T(2,128)S(1)}, f32[2,2048]{1,0:T(2,128)}, u32[]{:S(2)}) copy-start(f32[2,2048]{1,0:T(2,128)} %param.19) | copy-start | bytes 49156
  1.4 15.6 %collective-permute-start = (bf16[1,2048]{1,0:T(2,128)(2,1)S(1)}, bf16[1,2048]{1,0:T(2,128)(2,1)S(1)}, u32[]{:S(2)}, u32[]{:S(2)}) collective-permute-start(bf16[1,2048]{1,0:T(2,128)(2,1)S(1)} %slice.220), channel_id=1, source_target_pairs={{128,0},{136,8},{144,16},{152,24},{160,32},{168,40},{176,48},{184,... | collective-permute-start | bytes 12296 | tf_op jit(solution)/shard_map/ppermute | solution.py:14
  4.5 14.3 %collective-permute-start.1 = (bf16[1,2048]{1,0:T(2,128)(2,1)}, bf16[1,2048]{1,0:T(2,128)(2,1)S(1)}, u32[]{:S(2)}, u32[]{:S(2)}) collective-permute-start(bf16[1,2048]{1,0:T(2,128)(2,1)} %param.14), channel_id=1, source_target_pairs={{0,8},{8,0},{16,24},{24,16},{32,40},{40,32},{48,56},{56,48},{64,72... | collective-permute-start | bytes 12296 | tf_op jit(solution)/shard_map/ppermute | solution.py:20
  9.5 48.6 %collective-permute-start.2 = (bf16[2,2,2048,1,128]{4,2,1,0,3:T(8,128)(2,1)}, bf16[2,2,2048,1,128]{4,2,1,0,3:T(8,128)(2,1)}, u32[]{:S(2)}, u32[]{:S(2)}) collective-permute-start(bf16[2,2,2048,1,128]{4,2,1,0,3:T(8,128)(2,1)} %slice_bitcast_fusion), channel_id=1, source_target_pairs={{128,0},{136,8},{144,16},{152,24},{160,32},{168,40},{176,48},{184,... | collective-permute-start | bytes 6291464 | tf_op jit(solution)/shard_map/ppermute | solution.py:14
  11.9 3.1 %copy-start.2 = (bf16[3,2048]{1,0:T(4,128)(2,1)S(1)}, bf16[3,2048]{1,0:T(4,128)(2,1)}, u32[]{:S(2)}) copy-start(bf16[3,2048]{1,0:T(4,128)(2,1)} %param.13) | copy-start | bytes 36868
  15.0 3.8 %copy-start.3 = (bf16[1,2048]{1,0:T(2,128)(2,1)S(1)}, bf16[1,2048]{1,0:T(2,128)(2,1)}, u32[]{:S(2)}) copy-start(bf16[1,2048]{1,0:T(2,128)(2,1)} %param.14) | copy-start | bytes 12292
  18.5 6.0 %copy-start.8 = (bf16[2,2048,128]{2,1,0:T(8,128)(2,1)S(1)}, bf16[2,2048,128]{2,1,0:T(8,128)(2,1)}, u32[]{:S(2)}) copy-start(bf16[2,2048,128]{2,1,0:T(8,128)(2,1)} %param.24) | copy-start | bytes 3145732
  25.7 35.4 %copy-start = (bf16[2,256,2048]{2,1,0:T(8,128)(2,1)S(1)}, bf16[2,256,2048]{2,1,0:T(8,128)(2,1)}, u32[]{:S(2)}) copy-start(bf16[2,256,2048]{2,1,0:T(8,128)(2,1)} %param.25) | copy-start | bytes 6291460
  29.3 3.7 %collective-permute-start.5 = (f32[2,1,2]{2,0,1:T(2,128)S(1)}, f32[2,1,2]{2,0,1:T(2,128)S(1)}, u32[]{:S(2)}, u32[]{:S(2)}) collective-permute-start(f32[2,1,2]{2,0,1:T(2,128)S(1)} %bitcast.429), channel_id=1, source_target_pairs={{0,8},{8,0},{16,24},{24,16},{32,40},{40,32},{48,56},{56,48},{64,72... | collective-permute-start | bytes 56 | tf_op jit(solution)/shard_map/ppermute | solution.py:20
  29.5 3.6 %collective-permute-start.3 = (f32[2,1,2]{2,0,1:T(2,128)S(1)}, f32[2,1,2]{2,0,1:T(2,128)S(1)}, u32[]{:S(2)}, u32[]{:S(2)}) collective-permute-start(f32[2,1,2]{2,0,1:T(2,128)S(1)} %bitcast.428), channel_id=1, source_target_pairs={{0,8},{8,0},{16,24},{24,16},{32,40},{40,32},{48,56},{56,48},{64,72... | collective-permute-start | bytes 56 | tf_op jit(solution)/shard_map/ppermute | solution.py:20
  31.4 3.6 %collective-permute-start.4 = (f32[2,1,2,128]{3,2,0,1:T(2,128)S(1)}, f32[2,1,2,128]{3,2,0,1:T(2,128)S(1)}, u32[]{:S(2)}, u32[]{:S(2)}) collective-permute-start(f32[2,1,2,128]{3,2,0,1:T(2,128)S(1)} %bitcast.435), channel_id=1, source_target_pairs={{0,8},{8,0},{16,24},{24,16},{32,40},{40,32},{48,56},{56,48},{64,72... | collective-permute-start | bytes 6152 | tf_op jit(solution)/shard_map/ppermute | solution.py:20
  86.5 7.4 %copy-start.7 = (bf16[2,2,1,2,2048,1,128]{6,4,5,3,2,1,0:T(8,128)(2,1)S(1)}, bf16[2,2,1,2,2048,1,128]{6,4,5,3,2,1,0:T(8,128)(2,1)}, u32[]{:S(2)}) copy-start(bf16[2,2,1,2,2048,1,128]{6,4,5,3,2,1,0:T(8,128)(2,1)} %param.16) | copy-start | bytes 12582916
  103.2 3.7 %collective-permute-start.8 = (f32[2,1,2]{2,0,1:T(2,128)S(1)}, f32[2,1,2]{2,0,1:T(2,128)S(1)}, u32[]{:S(2)}, u32[]{:S(2)}) collective-permute-start(f32[2,1,2]{2,0,1:T(2,128)S(1)} %bitcast.427), channel_id=1, source_target_pairs={{0,8},{8,0},{16,24},{24,16},{32,40},{40,32},{48,56},{56,48},{64,72... | collective-permute-start | bytes 56 | tf_op jit(solution)/shard_map/ppermute | solution.py:20
  103.7 3.6 %collective-permute-start.6 = (f32[2,1,2]{2,0,1:T(2,128)S(1)}, f32[2,1,2]{2,0,1:T(2,128)S(1)}, u32[]{:S(2)}, u32[]{:S(2)}) collective-permute-start(f32[2,1,2]{2,0,1:T(2,128)S(1)} %bitcast.426), channel_id=1, source_target_pairs={{0,8},{8,0},{16,24},{24,16},{32,40},{40,32},{48,56},{56,48},{64,72... | collective-permute-start | bytes 56 | tf_op jit(solution)/shard_map/ppermute | solution.py:20
  105.3 3.6 %collective-permute-start.7 = (f32[2,1,2,128]{3,2,0,1:T(2,128)S(1)}, f32[2,1,2,128]{3,2,0,1:T(2,128)S(1)}, u32[]{:S(2)}, u32[]{:S(2)}) collective-permute-start(f32[2,1,2,128]{3,2,0,1:T(2,128)S(1)} %bitcast.434), channel_id=1, source_target_pairs={{0,8},{8,0},{16,24},{24,16},{32,40},{40,32},{48,56},{56,48},{64,72... | collective-permute-start | bytes 6152 | tf_op jit(solution)/shard_map/ppermute | solution.py:20
where the time goes:
time: 138 us
  blocking collectives  48.8 us (35%)
  waiting for transfers between devices  28.8 us (21%)
  matrix products  27.8 us (20%)
  local copies, waits for them, and re-layouts  13.2 us (10%)
  starting transfers between devices  10.3 us (7%)
  other arithmetic  5.61 us (4%)
  between operations  3.04 us (2%)
    psum x2, blocking collectives, local(): summed = lax.psum(heads_out, 'tensor')  48.8 us
    ppermute x2, waiting for transfers between devices, shifted(): return lax.ppermute(block, axis, route)  23.1 us
    dot_general x6, matrix products, masked_scores(): jnp.einsum('kgd,tkd->kgt', grouped, key_rows, preferred_element_type=jnp....  8.49 us
    ppermute x7, starting transfers between devices, partner_2(): return lax.ppermute(value, axis, pairs)  6.68 us
    ppermute x7, waiting for transfers between devices, partner_2(): return lax.ppermute(value, axis, pairs)  5.76 us
    dot_general x4, matrix products, attend(): jnp.einsum('kgt,tkd->kgd', weights.astype(jnp.bfloat16), value_rows, pref...  5.64 us
    dot_general x4, matrix products, project(): jnp.dot(normed, key_weight, preferred_element_type=jnp.float32)  5.57 us
    ppermute x2, starting transfers between devices, shifted(): return lax.ppermute(block, axis, route)  3.62 us
  transfers between devices with their start and end apart: 9, of which 7 were waited for; matrix products, arithmetic and copies ran while one was open for 15% of the time, Pallas kernels for 0%

commit v1 on v0

--- a/solution.py
+++ b/solution.py
@@ -224,7 +224,7 @@
             w_out[layer_at],
             preferred_element_type=jnp.float32,
         )
-        summed = lax.psum(heads_out, "tensor")
+        summed = jnp.sum(lax.all_gather(heads_out, "tensor"), axis=0)
         carried = jnp.concatenate([hidden, long_hidden], axis=0).astype(jnp.float32) + summed
         if layer_at + 1 < layers:
             carried = carried.astype(jnp.bfloat16)

time: 138 us -> 120 us (0.87); the launches traced: 138 us -> 118 us
  blocking collectives: 48.8 us -> 27.8 us
    psum x2 -> x0, blocking collectives: 48.8 us -> none  [local(): summed = lax.psum(heads_out, 'tensor')]
    all_gather x0 -> x2, blocking collectives: none -> 27.8 us  [local(): summed = jnp.sum(lax.all_gather(heads_out, 'tensor'), axis=0)]
  transfers between devices with their start and end apart: 9 -> 9, of which waited for: 7 -> 7; matrix products, arithmetic and copies ran while one was open for 15% -> 18% of each run, Pallas kernels for 0% -> 0%
where the time goes in v1:
time: 120 us; the launch traced here: 118 us
  waiting for transfers between devices  29 us (24%)
  matrix products  27.8 us (23%)
  blocking collectives  27.8 us (23%)
  local copies, waits for them, and re-layouts  13.2 us (11%)
  starting transfers between devices  10.1 us (8%)
  other arithmetic  6.74 us (6%)
  between operations  3.03 us (3%)
    all_gather x2, blocking collectives, local(): summed = jnp.sum(lax.all_gather(heads_out, 'tensor'), axis=0)  27.8 us
    ppermute x2, waiting for transfers between devices, shifted(): return lax.ppermute(block, axis, route)  23.1 us
    dot_general x6, matrix products, masked_scores(): jnp.einsum('kgd,tkd->kgt', grouped, key_rows, preferred_element_type=jnp....  8.49 us
    ppermute x7, starting transfers between devices, partner_2(): return lax.ppermute(value, axis, pairs)  6.51 us
    ppermute x7, waiting for transfers between devices, partner_2(): return lax.ppermute(value, axis, pairs)  5.93 us
    dot_general x4, matrix products, attend(): jnp.einsum('kgt,tkd->kgd', weights.astype(jnp.bfloat16), value_rows, pref...  5.64 us
    dot_general x4, matrix products, project(): jnp.dot(normed, key_weight, preferred_element_type=jnp.float32)  5.57 us
    ppermute x2, starting transfers between devices, shifted(): return lax.ppermute(block, axis, route)  3.62 us
  transfers between devices with their start and end apart: 9, of which 7 were waited for; matrix products, arithmetic and copies ran while one was open for 18% of the time, Pallas kernels for 0%

profile of v1, /device:TPU:64, one launch (start us, length us, event | category | flops | bytes accessed | tf_op | source)
XLA Modules:
  0.0 117.7 jit_solution(5312890221545724412)
XLA Ops:
  1.4 3.1 %collective-permute-start = (bf16[1,2048]{1,0:T(2,128)(2,1)S(1)}, bf16[1,2048]{1,0:T(2,128)(2,1)S(1)}, u32[]{:S(2)}, u32[]{:S(2)}) collective-permute-start(bf16[1,2048]{1,0:T(2,128)(2,1)S(1)} %slice.220), channel_id=1, source_target_pairs={{128,0},{136,8},{144,16},{152,24},{160,32},{168,40},{176,48},{184,... | collective-permute-start | bytes 12296 | tf_op jit(solution)/shard_map/ppermute | solution.py:14
  4.5 1.9 %collective-permute-start.1 = (bf16[1,2048]{1,0:T(2,128)(2,1)}, bf16[1,2048]{1,0:T(2,128)(2,1)S(1)}, u32[]{:S(2)}, u32[]{:S(2)}) collective-permute-start(bf16[1,2048]{1,0:T(2,128)(2,1)} %param.14), channel_id=1, source_target_pairs={{0,8},{8,0},{16,24},{24,16},{32,40},{40,32},{48,56},{56,48},{64,72... | collective-permute-start | bytes 12296 | tf_op jit(solution)/shard_map/ppermute | solution.py:20
  6.5 3.0 %slice_bitcast_fusion = bf16[2,2,2048,1,128]{4,2,1,0,3:T(8,128)(2,1)} fusion(bf16[2,2,3,2048,1,128]{5,3,4,2,1,0:T(8,128)(2,1)} %param.15), kind=kLoop, calls=%fused_computation.14 | loop fusion | bytes 4194304 | tf_op jit(solution)/shard_map/squeeze | solution.py:158
  11.9 1.7 %slice_bitcast_fusion.18 = (bf16[256,2048]{0,1:T(8,128)(2,1)S(1)}, bf16[256,2048]{0,1:T(8,128)(2,1)S(1)}) fusion(bf16[2,2048,256]{2,1,0:T(8,128)(2,1)} %param.22), kind=kLoop, calls=%fused_computation.56 | loop fusion | bytes 4194304 | tf_op jit(solution)/shard_map/dot_general | solution.py:47
  17.2 1.4 %multiply_reduce_fusion.5 = (f32[3]{0:T(128)S(1)}, f32[3,128]{1,0:T(4,128)S(1)}) fusion(bf16[2,2048,128]{2,1,0:T(8,128)(2,1)} %param.23, f32[2048]{0:T(1024)S(1)} %bitcast.418, f32[3]{0:T(128)S(1)} %add_rsqrt_fusion.11, bf16[1,2048]{1,0:T(2,128)(2,1)S(1)} %collective-permute-done, bf16[2,2048]{1,0:T(2,128)(2,1)S(1)} %slice.219), kind=kOutput, calls=%fused_computation.200 | convolution fusion | flops 1616637 | bytes 546328 | tf_op jit(solution)/shard_map/dot_general | solution.py:50
  21.1 1.7 %fusion.201 = (f32[2,2]{1,0:T(2,128)S(1)}, f32[2,2,2048]{2,1,0:T(2,128)S(1)}) fusion(bf16[2,2,1,2,2048,1,128]{6,4,3,5,2,1,0:T(8,128)(2,1)} %bitcast.445, bf16[2,2,128]{2,0,1:T(2,128)(2,1)S(1)} %pad_maximum_fusion.4, pred[2,2048]{1,0:T(4,128)(4,1)S(1)} %broadcast_compare_fusion), kind=kOutput, calls=%fused_computation.350 | convolution fusion | flops 2121724 | bytes 1086480 | tf_op jit(solution)/shard_map/vmap(kgd,tkd->kgt)/dot_general | solution.py:74
  23.0 1.5 %fusion.23 = f32[2,2,128]{2,1,0:T(2,128)S(1)} fusion(bf16[2,2,1,2,2048,1,128]{6,4,3,5,2,1,0:T(8,128)(2,1)} %bitcast.446, f32[2,2,2048]{2,1,0:T(2,128)S(1)} %get-tuple-element.64, f32[2,2]{1,0:T(2,128)S(1)} %get-tuple-element.63), kind=kOutput, calls=%fused_computation.47 | convolution fusion | flops 2113536 | bytes 1083408 | tf_op jit(solution)/shard_map/vmap(kgt,tkd->kgd)/dot_general | solution.py:99
  25.7 1.8 %fusion.203 = (f32[2,2]{1,0:T(2,128)S(1)}, f32[2,2,2048]{2,1,0:T(2,128)S(1)}) fusion(bf16[2,2,3,2048,1,128]{5,3,2,4,1,0:T(8,128)(2,1)} %bitcast.408, bf16[2,2,128]{2,0,1:T(2,128)(2,1)S(1)} %fusion.141, pred[2,2048]{1,0:T(4,128)(4,1)S(1)} %bitcast.424), kind=kOutput, calls=%fused_computation.352 | convolution fusion | flops 2121724 | bytes 1086480 | tf_op jit(solution)/shard_map/vmap(kgd,tkd->kgt)/dot_general | solution.py:74
  27.7 1.5 %fusion.11 = bf16[1,2,2,128]{3,2,1,0:T(2,128)(2,1)S(1)} fusion(bf16[2,2,3,2048,1,128]{5,3,2,4,1,0:T(8,128)(2,1)} %bitcast.409, f32[2,2,2048]{2,1,0:T(2,128)S(1)} %get-tuple-element.72, f32[2,2]{1,0:T(2,128)S(1)} %multiply_maximum_fusion.1, f32[2,2]{1,0:T(2,128)S(1)} %get-tuple-element.42, f32[2,128]{1,0:T(2,128)S(1)} %slice_convert_fusion.1, ...), kind=kOutput, calls=%fused_computation.24 | convolution fusion | flops 2115584 | bytes 1083440 | tf_op jit(solution)/shard_map/vmap(kgt,tkd->kgd)/dot_general | solution.py:87
  29.5 1.9 %collective-permute-start.3 = (f32[2,1,2]{2,0,1:T(2,128)S(1)}, f32[2,1,2]{2,0,1:T(2,128)S(1)}, u32[]{:S(2)}, u32[]{:S(2)}) collective-permute-start(f32[2,1,2]{2,0,1:T(2,128)S(1)} %bitcast.432), channel_id=1, source_target_pairs={{0,8},{8,0},{16,24},{24,16},{32,40},{40,32},{48,56},{56,48},{64,72... | collective-permute-start | bytes 56 | tf_op jit(solution)/shard_map/ppermute | solution.py:20
  33.1 1.9 %collective-permute-done.4 = f32[2,1,2,128]{3,2,0,1:T(2,128)S(1)} collective-permute-done((f32[2,1,2,128]{3,2,0,1:T(2,128)S(1)}, f32[2,1,2,128]{3,2,0,1:T(2,128)S(1)}, u32[]{:S(2)}, u32[]{:S(2)}) %collective-permute-start.4) | collective-permute-done | bytes 2080 | tf_op jit(solution)/shard_map/ppermute | solution.py:20
  35.1 23.0 %collective-permute-done.2 = bf16[2,2,2048,1,128]{4,2,1,0,3:T(8,128)(2,1)} collective-permute-done((bf16[2,2,2048,1,128]{4,2,1,0,3:T(8,128)(2,1)}, bf16[2,2,2048,1,128]{4,2,1,0,3:T(8,128)(2,1)}, u32[]{:S(2)}, u32[]{:S(2)}) %collective-permute-start.2) | collective-permute-done | bytes 2097184 | tf_op jit(solution)/shard_map/ppermute | solution.py:14
  58.1 1.4 %fusion.202 = (f32[2]{0:T(128)S(1)}, f32[2,2048]{1,0:T(2,128)S(1)}) fusion(bf16[2,2,2048,1,128]{4,2,1,0,3:T(8,128)(2,1)} %collective-permute-done.2, bf16[1,2,128]{2,0,1:T(2,128)(2,1)S(1)} %pad_maximum_fusion.2, pred[2048]{0:T(1024)(128)(4,1)S(1)} %slice_reduce_fusion), kind=kOutput, calls=%fused_computation.351 | convolution fusion | flops 1060862 | bytes 543240 | tf_op jit(solution)/shard_map/kgd,tkd->kgt/dot_general | solution.py:74
  61.3 14.7 %all-gather.2 = f32[8,5,2048]{2,1,0:T(8,128)} all-gather(f32[1,5,2048]{2,1,0:T(8,128)S(1)} %convolution_bitcast_fusion.1), channel_id=2, replica_groups=mesh['replica'=32,'tensor'=8] {'tensor'}, dimensions={0}, use_global_device_ids=true | all-gather | bytes 368640 | tf_op jit(solution)/shard_map/all_gather | solution.py:227
  77.4 1.4 %convolution_convert_fusion = bf16[3,128]{1,0:T(4,128)(2,1)S(1)} fusion(bf16[2,2048,128]{2,1,0:T(8,128)(2,1)} %param.24, f32[2048]{0:T(1024)S(1)} %bitcast.412, f32[3]{0:T(128)S(1)} %add_rsqrt_fusion.7, bf16[5,2048]{1,0:T(8,128)(2,1)S(1)} %add_convert_fusion), kind=kOutput, calls=%fused_computation.19 | convolution fusion | flops 1597824 | bytes 550144 | tf_op jit(solution)/shard_map/dot_general | solution.py:54
  80.2 1.4 %multiply_reduce_fusion.6 = (f32[2]{0:T(128)S(1)}, f32[2,128]{1,0:T(2,128)S(1)}) fusion(bf16[2,2048,128]{2,1,0:T(8,128)(2,1)} %param.23, f32[2]{0:T(128)S(1)} %add_rsqrt_fusion.5, f32[2048]{0:T(1024)S(1)} %bitcast.414, bf16[5,2048]{1,0:T(8,128)(2,1)S(1)} %add_convert_fusion), kind=kOutput, calls=%fused_computation.244 | convolution fusion | flops 1065470 | bytes 542216 | tf_op jit(solution)/shard_map/dot_general | solution.py:50
  82.5 1.4 %multiply_reduce_fusion.3 = (f32[3]{0:T(128)S(1)}, f32[3,128]{1,0:T(4,128)S(1)}) fusion(bf16[2,2048,128]{2,1,0:T(8,128)(2,1)} %param.23, f32[2048]{0:T(1024)S(1)} %bitcast.417, f32[3]{0:T(128)S(1)} %add_rsqrt_fusion.7, bf16[5,2048]{1,0:T(8,128)(2,1)S(1)} %add_convert_fusion), kind=kOutput, calls=%fused_computation.194 | convolution fusion | flops 1598205 | bytes 550924 | tf_op jit(solution)/shard_map/dot_general | solution.py:50
  86.3 1.7 %fusion.206 = (f32[2,2]{1,0:T(2,128)S(1)}, f32[2,2,2048]{2,1,0:T(2,128)S(1)}) fusion(bf16[2,2,3,2048,1,128]{5,3,2,4,1,0:T(8,128)(2,1)} %bitcast.410, bf16[2,2,128]{2,0,1:T(2,128)(2,1)S(1)} %fusion.140, pred[2,2048]{1,0:T(4,128)(4,1)S(1)} %bitcast.425), kind=kOutput, calls=%fused_computation.355 | convolution fusion | flops 2121724 | bytes 1086480 | tf_op jit(solution)/shard_map/vmap(kgd,tkd->kgt)/dot_general | solution.py:74
  88.1 1.4 %fusion.205 = (f32[2]{0:T(128)S(1)}, f32[2,2048]{1,0:T(2,128)S(1)}) fusion(bf16[2,2,2048,1,128]{4,2,1,0,3:T(8,128)(2,1)} %collective-permute-done.2, bf16[1,2,128]{2,0,1:T(2,128)(2,1)S(1)} %pad_maximum_fusion.1, pred[2048]{0:T(1024)(128)(4,1)S(1)} %slice_reduce_fusion), kind=kOutput, calls=%fused_computation.354 | convolution fusion | flops 1060862 | bytes 543240 | tf_op jit(solution)/shard_map/kgd,tkd->kgt/dot_general | solution.py:74
  92.6 1.5 %fusion.10 = bf16[1,2,2,128]{3,2,1,0:T(2,128)(2,1)S(1)} fusion(bf16[2,2,3,2048,1,128]{5,3,2,4,1,0:T(8,128)(2,1)} %bitcast.411, f32[2,2,2048]{2,1,0:T(2,128)S(1)} %get-tuple-element.86, f32[2,2]{1,0:T(2,128)S(1)} %multiply_maximum_fusion, f32[2,2]{1,0:T(2,128)S(1)} %get-tuple-element.36, f32[2,128]{1,0:T(2,128)S(1)} %slice_convert_fusion, ...), kind=kOutput, calls=%fused_computation.23 | convolution fusion | flops 2115584 | bytes 1083440 | tf_op jit(solution)/shard_map/vmap(kgt,tkd->kgd)/dot_general | solution.py:87
  94.5 1.8 %collective-permute-start.6 = (f32[2,1,2]{2,0,1:T(2,128)S(1)}, f32[2,1,2]{2,0,1:T(2,128)S(1)}, u32[]{:S(2)}, u32[]{:S(2)}) collective-permute-start(f32[2,1,2]{2,0,1:T(2,128)S(1)} %bitcast.430), channel_id=1, source_target_pairs={{0,8},{8,0},{16,24},{24,16},{32,40},{40,32},{48,56},{56,48},{64,72... | collective-permute-start | bytes 56 | tf_op jit(solution)/shard_map/ppermute | solution.py:20
  98.1 1.8 %collective-permute-done.7 = f32[2,1,2,128]{3,2,0,1:T(2,128)S(1)} collective-permute-done((f32[2,1,2,128]{3,2,0,1:T(2,128)S(1)}, f32[2,1,2,128]{3,2,0,1:T(2,128)S(1)}, u32[]{:S(2)}, u32[]{:S(2)}) %collective-permute-start.7) | collective-permute-done | bytes 2080 | tf_op jit(solution)/shard_map/ppermute | solution.py:20
  100.2 13.1 %all-gather.3 = f32[8,5,2048]{2,1,0:T(8,128)S(1)} all-gather(f32[1,5,2048]{2,1,0:T(8,128)S(1)} %convolution_bitcast_fusion), channel_id=3, replica_groups=mesh['replica'=32,'tensor'=8] {'tensor'}, dimensions={0}, use_global_device_ids=true | all-gather | bytes 368640 | tf_op jit(solution)/shard_map/all_gather | solution.py:227
  114.6 3.0 %copy.143 = bf16[1,2,2,2048,1,128]{5,3,4,2,1,0:T(8,128)(2,1)} copy(bf16[1,2,2,2048,1,128]{5,3,4,2,1,0:T(8,128)(2,1)} %dynamic_update_slice.4) | data formatting | bytes 4194304
  (160 shorter events, 25.4 us)
Async XLA Ops:
  1.4 8.7 %copy-start.9 = (s32[96]{0:T(128)S(1)}, s32[96]{0:T(128)}, u32[]{:S(2)}) copy-start(s32[96]{0:T(128)} %param.17) | copy-start | bytes 1156
  1.4 9.3 %copy-start.4 = (f32[2,128]{1,0:T(2,128)S(1)}, f32[2,128]{1,0:T(2,128)}, u32[]{:S(2)}) copy-start(f32[2,128]{1,0:T(2,128)} %param.20) | copy-start | bytes 3076
  1.4 9.3 %copy-start.5 = (f32[2,128]{1,0:T(2,128)S(1)}, f32[2,128]{1,0:T(2,128)}, u32[]{:S(2)}) copy-start(f32[2,128]{1,0:T(2,128)} %param.21) | copy-start | bytes 3076
  1.4 10.0 %copy-start.6 = (s32[32]{0:T(128)S(1)}, s32[32]{0:T(128)}, u32[]{:S(2)}) copy-start(s32[32]{0:T(128)} %param.18) | copy-start | bytes 388
  1.4 10.4 %copy-start.1 = (f32[2,2048]{1,0:T(2,128)S(1)}, f32[2,2048]{1,0:T(2,128)}, u32[]{:S(2)}) copy-start(f32[2,2048]{1,0:T(2,128)} %param.19) | copy-start | bytes 49156
  1.4 15.6 %collective-permute-start = (bf16[1,2048]{1,0:T(2,128)(2,1)S(1)}, bf16[1,2048]{1,0:T(2,128)(2,1)S(1)}, u32[]{:S(2)}, u32[]{:S(2)}) collective-permute-start(bf16[1,2048]{1,0:T(2,128)(2,1)S(1)} %slice.220), channel_id=1, source_target_pairs={{128,0},{136,8},{144,16},{152,24},{160,32},{168,40},{176,48},{184,... | collective-permute-start | bytes 12296 | tf_op jit(solution)/shard_map/ppermute | solution.py:14
  4.5 14.3 %collective-permute-start.1 = (bf16[1,2048]{1,0:T(2,128)(2,1)}, bf16[1,2048]{1,0:T(2,128)(2,1)S(1)}, u32[]{:S(2)}, u32[]{:S(2)}) collective-permute-start(bf16[1,2048]{1,0:T(2,128)(2,1)} %param.14), channel_id=1, source_target_pairs={{0,8},{8,0},{16,24},{24,16},{32,40},{40,32},{48,56},{56,48},{64,72... | collective-permute-start | bytes 12296 | tf_op jit(solution)/shard_map/ppermute | solution.py:20
  9.5 48.6 %collective-permute-start.2 = (bf16[2,2,2048,1,128]{4,2,1,0,3:T(8,128)(2,1)}, bf16[2,2,2048,1,128]{4,2,1,0,3:T(8,128)(2,1)}, u32[]{:S(2)}, u32[]{:S(2)}) collective-permute-start(bf16[2,2,2048,1,128]{4,2,1,0,3:T(8,128)(2,1)} %slice_bitcast_fusion), channel_id=1, source_target_pairs={{128,0},{136,8},{144,16},{152,24},{160,32},{168,40},{176,48},{184,... | collective-permute-start | bytes 6291464 | tf_op jit(solution)/shard_map/ppermute | solution.py:14
  11.9 3.1 %copy-start.2 = (bf16[3,2048]{1,0:T(4,128)(2,1)S(1)}, bf16[3,2048]{1,0:T(4,128)(2,1)}, u32[]{:S(2)}) copy-start(bf16[3,2048]{1,0:T(4,128)(2,1)} %param.13) | copy-start | bytes 36868
  15.0 3.8 %copy-start.3 = (bf16[1,2048]{1,0:T(2,128)(2,1)S(1)}, bf16[1,2048]{1,0:T(2,128)(2,1)}, u32[]{:S(2)}) copy-start(bf16[1,2048]{1,0:T(2,128)(2,1)} %param.14) | copy-start | bytes 12292
  18.5 6.0 %copy-start.8 = (bf16[2,2048,128]{2,1,0:T(8,128)(2,1)S(1)}, bf16[2,2048,128]{2,1,0:T(8,128)(2,1)}, u32[]{:S(2)}) copy-start(bf16[2,2048,128]{2,1,0:T(8,128)(2,1)} %param.24) | copy-start | bytes 3145732
  25.7 35.4 %copy-start = (bf16[2,256,2048]{2,1,0:T(8,128)(2,1)S(1)}, bf16[2,256,2048]{2,1,0:T(8,128)(2,1)}, u32[]{:S(2)}) copy-start(bf16[2,256,2048]{2,1,0:T(8,128)(2,1)} %param.25) | copy-start | bytes 6291460
  29.3 3.7 %collective-permute-start.5 = (f32[2,1,2]{2,0,1:T(2,128)S(1)}, f32[2,1,2]{2,0,1:T(2,128)S(1)}, u32[]{:S(2)}, u32[]{:S(2)}) collective-permute-start(f32[2,1,2]{2,0,1:T(2,128)S(1)} %bitcast.433), channel_id=1, source_target_pairs={{0,8},{8,0},{16,24},{24,16},{32,40},{40,32},{48,56},{56,48},{64,72... | collective-permute-start | bytes 56 | tf_op jit(solution)/shard_map/ppermute | solution.py:20
  29.5 3.6 %collective-permute-start.3 = (f32[2,1,2]{2,0,1:T(2,128)S(1)}, f32[2,1,2]{2,0,1:T(2,128)S(1)}, u32[]{:S(2)}, u32[]{:S(2)}) collective-permute-start(f32[2,1,2]{2,0,1:T(2,128)S(1)} %bitcast.432), channel_id=1, source_target_pairs={{0,8},{8,0},{16,24},{24,16},{32,40},{40,32},{48,56},{56,48},{64,72... | collective-permute-start | bytes 56 | tf_op jit(solution)/shard_map/ppermute | solution.py:20
  31.4 3.6 %collective-permute-start.4 = (f32[2,1,2,128]{3,2,0,1:T(2,128)S(1)}, f32[2,1,2,128]{3,2,0,1:T(2,128)S(1)}, u32[]{:S(2)}, u32[]{:S(2)}) collective-permute-start(f32[2,1,2,128]{3,2,0,1:T(2,128)S(1)} %bitcast.439), channel_id=1, source_target_pairs={{0,8},{8,0},{16,24},{24,16},{32,40},{40,32},{48,56},{56,48},{64,72... | collective-permute-start | bytes 6152 | tf_op jit(solution)/shard_map/ppermute | solution.py:20
  77.4 7.4 %copy-start.7 = (bf16[2,2,1,2,2048,1,128]{6,4,5,3,2,1,0:T(8,128)(2,1)S(1)}, bf16[2,2,1,2,2048,1,128]{6,4,5,3,2,1,0:T(8,128)(2,1)}, u32[]{:S(2)}) copy-start(bf16[2,2,1,2,2048,1,128]{6,4,5,3,2,1,0:T(8,128)(2,1)} %param.16) | copy-start | bytes 12582916
  94.2 3.7 %collective-permute-start.8 = (f32[2,1,2]{2,0,1:T(2,128)S(1)}, f32[2,1,2]{2,0,1:T(2,128)S(1)}, u32[]{:S(2)}, u32[]{:S(2)}) collective-permute-start(f32[2,1,2]{2,0,1:T(2,128)S(1)} %bitcast.431), channel_id=1, source_target_pairs={{0,8},{8,0},{16,24},{24,16},{32,40},{40,32},{48,56},{56,48},{64,72... | collective-permute-start | bytes 56 | tf_op jit(solution)/shard_map/ppermute | solution.py:20
  94.5 3.6 %collective-permute-start.6 = (f32[2,1,2]{2,0,1:T(2,128)S(1)}, f32[2,1,2]{2,0,1:T(2,128)S(1)}, u32[]{:S(2)}, u32[]{:S(2)}) collective-permute-start(f32[2,1,2]{2,0,1:T(2,128)S(1)} %bitcast.430), channel_id=1, source_target_pairs={{0,8},{8,0},{16,24},{24,16},{32,40},{40,32},{48,56},{56,48},{64,72... | collective-permute-start | bytes 56 | tf_op jit(solution)/shard_map/ppermute | solution.py:20
  96.3 3.6 %collective-permute-start.7 = (f32[2,1,2,128]{3,2,0,1:T(2,128)S(1)}, f32[2,1,2,128]{3,2,0,1:T(2,128)S(1)}, u32[]{:S(2)}, u32[]{:S(2)}) collective-permute-start(f32[2,1,2,128]{3,2,0,1:T(2,128)S(1)} %bitcast.438), channel_id=1, source_target_pairs={{0,8},{8,0},{16,24},{24,16},{32,40},{40,32},{48,56},{56,48},{64,72... | collective-permute-start | bytes 6152 | tf_op jit(solution)/shard_map/ppermute | solution.py:20
